TPU v7x, 32 devices: a whole 2x2x4 slice. The times are simulated.
32 devices in a mesh: row: 4 (over y, core), col: 8 (over z, x).
Axes of the slice: x: 2, y: 2, z: 4, core: 2. Of those that a mesh axis runs over, the one named last changes fastest.
Arguments:
- hess_inv: float32 [16384, 16384], P('row', 'col'), as said below
- weights: bfloat16 [6144, 16384], P('row', 'col'), may hold values from -6 to 6
- removed: int32 [128], replicated, may hold values from 0 to 16383, as said below
Outputs:
- hess_out: float32 [16384, 16384], P('row', 'col')
- weight_out: bfloat16 [6144, 16384], P('row', 'col')
Inputs may be any that keep to these rules, and one draw needn't show every extreme that they name: `removed`: sorted ascending and distinct; each aligned block of 2048 columns holds at most 48 of them, and at least one block holds exactly 48. `hess_inv`: symmetric and positive definite.
All inputs are finite; a program needn't handle non-finite values.
Results may differ from a plain program's by a relative error of at most 0.005.
Values may be sent and summed in bfloat16 or wider, within the bound.
No kernel may reach another device: no remote copies, remote signals or barrier semaphores. Data moves between devices by JAX's collectives and lax.ppermute only.
A program may use at most 128 MiB of HBM per device.

v0:
```python
import jax
import jax.numpy as jnp
from jax import lax
from jax.sharding import PartitionSpec as P

MOST = 48


def spread(block, axis, owner):
    block = jnp.where(lax.axis_index(axis) == owner, block, jnp.zeros_like(block))
    return lax.psum(block, axis)


def pick_owned(source, removed, tile_index, tile_size, slot_count, which_axis):
    before = jnp.sum((removed < tile_index * tile_size).astype(jnp.int32))
    within = jnp.sum((removed // tile_size == tile_index).astype(jnp.int32))
    slot_rank = jnp.arange(slot_count, dtype=jnp.int32)
    chosen = jnp.clip(before + slot_rank, 0, removed.shape[0] - 1)
    local_col = jnp.clip(removed[chosen] - tile_index * tile_size, 0, tile_size - 1)
    taken_part = jnp.take(source, local_col, axis=which_axis)
    live_slot = slot_rank < within
    mask_shape = [1, 1]
    mask_shape[which_axis] = slot_count
    return jnp.where(live_slot.reshape(mask_shape), taken_part, jnp.zeros((), taken_part.dtype))


def slot_map(removed, tile_size, slot_count):
    which_tile = removed // tile_size
    first_pos = jnp.sum(
        (removed[None, :] < (which_tile * tile_size)[:, None]).astype(jnp.int32), axis=1
    )
    position = jnp.arange(removed.shape[0], dtype=jnp.int32)
    return which_tile * slot_count + position - first_pos


def on_device(hess_inv, weights, removed):
    row_count = lax.axis_size("row")
    col_count = lax.axis_size("col")
    row_index = lax.axis_index("row")
    col_index = lax.axis_index("col")
    row_tile, col_tile = hess_inv.shape
    tile_ratio = col_count // row_count
    col_slots = slot_map(removed, col_tile, MOST)
    packed_weight = pick_owned(weights, removed, col_index, col_tile, MOST, 1)
    packed_rows = pick_owned(hess_inv, removed, row_index, row_tile, tile_ratio * MOST, 0)
    gathered = lax.all_gather(packed_rows, "row", axis=0, tiled=True)
    upper_rows = jnp.take(gathered, slot_map(removed, row_tile, tile_ratio * MOST), axis=0)
    pieces = [
        spread(upper_rows.astype(jnp.bfloat16), "col", row_index * tile_ratio + offset).astype(
            upper_rows.dtype
        )
        for offset in range(tile_ratio)
    ]
    left_rows = jnp.concatenate(pieces, axis=1)
    weight_wide = lax.all_gather(packed_weight, "col", axis=1, tiled=True)
    weight_left = jnp.take(weight_wide, col_slots, axis=1)
    own_cols = pick_owned(upper_rows, removed, col_index, col_tile, MOST, 1)
    block_wide = lax.all_gather(own_cols, "col", axis=1, tiled=True)
    removed_block = jnp.take(block_wide, col_slots, axis=1)
    factor = jnp.linalg.cholesky(removed_block)
    identity = jnp.eye(removed_block.shape[0], dtype=jnp.float32)
    factor_inv = jax.scipy.linalg.solve_triangular(factor, identity, lower=True)
    block_inv = jnp.dot(factor_inv.T, factor_inv, precision=lax.Precision.HIGHEST)
    coupling = jnp.dot(block_inv, upper_rows, precision=lax.Precision.HIGHEST)
    correction = lax.dot_general(
        left_rows, coupling, (((0,), (0,)), ((), ())), precision=lax.Precision.HIGHEST
    )
    hess_out = hess_inv - correction
    weight_fix = jnp.dot(weight_left.astype(jnp.float32), coupling, precision=lax.Precision.HIGHEST)
    weight_out = (weights.astype(jnp.float32) - weight_fix).astype(jnp.bfloat16)
    return (hess_out, weight_out)


def solution(mesh):
    placed = (P("row", "col"), P("row", "col"), P())
    return jax.shard_map(
        on_device,
        mesh=mesh,
        in_specs=placed,
        out_specs=(P("row", "col"), P("row", "col")),
        check_vma=False,
    )
```

profile of v0, /device:TPU:0, one launch (start us, length us, event | category | flops | bytes accessed | tf_op | source)
XLA Modules:
  0.0 271.6 jit_solution(3088426548601150920)
XLA Ops:
  7.2 1.4 fusion.12
  9.3 1.4 gather_fusion.3
  10.8 0.7 iota_compare_fusion.3
  11.4 8.6 %copy.13 = bf16[1536,2048]{0,1:T(8,128)(2,1)} copy(bf16[1536,2048]{1,0:T(8,128)(2,1)} %param.4) | data formatting | bytes 12582912 | tf_op args[1]
  20.0 4.4 %gather_fusion.6 = bf16[48,1536]{1,0:T(8,128)(2,1)S(1)} fusion(bf16[1536,2048]{0,1:T(8,128)(2,1)} %copy.13, s32[1024]{0:T(1024)S(1)} %pad_clamp_fusion.1), kind=kCustom, calls=%fused_computation.6 | custom fusion | bytes 295104 | tf_op jit(solution)/shard_map/jit(_take)/gather | solution.py:20
  24.4 0.8 select_bitcast_fusion
  25.3 0.7 fusion.14
  26.0 1.2 gather_fusion
  27.3 11.9 %gather_fusion.1 = f32[96,2048]{1,0:T(8,128)S(1)} fusion(f32[4096,2048]{1,0:T(8,128)} %param.3, s32[1024]{0:T(1024)S(1)} %pad_clamp_fusion.4), kind=kCustom, calls=%fused_computation.1 | custom fusion | bytes 1573248 | tf_op jit(solution)/shard_map/jit(_take)/gather | solution.py:20
  40.5 1.0 select_select_fusion
  41.9 27.4 %all-gather.5.cloned.1.call-done = bf16[1536,384]{0,1:T(8,128)(2,1)} async-done(((bf16[1536,48]{0,1:T(8,128)(2,1)}), bf16[1536,384]{0,1:T(8,128)(2,1)}) %all-gather.5.cloned.1.call-update) | async-done | bytes 1179664 | tf_op jit(solution)/shard_map/all_gather | solution.py:55
  69.2 2.7 gather_fusion.7
  71.9 26.7 %all-gather.3.cloned.1.call-done = f32[384,2048]{1,0:T(8,128)} async-done(((f32[96,2048]{1,0:T(8,128)}), f32[384,2048]{1,0:T(8,128)}) %all-gather.3.cloned.1.call-update) | async-done | bytes 3145744 | tf_op jit(solution)/shard_map/all_gather | solution.py:46
  98.6 3.3 %gather_fusion.2 = f32[128,2048]{1,0:T(8,128)S(1)} fusion(f32[384,2048]{1,0:T(8,128)} %all-gather.3.cloned.1.call-done, s32[1024]{0:T(1024)S(1)} %pad_clamp_fusion.3), kind=kCustom, calls=%fused_computation.2 | custom fusion | bytes 2097664 | tf_op jit(solution)/shard_map/jit(_take)/gather | solution.py:47
  101.9 1.0 broadcast_select_fusion.2
  103.2 0.9 broadcast_select_fusion.1
  104.8 30.9 %all_gather.10 = f32[128,384]{0,1:T(8,128)S(1)} all-gather(f32[128,48]{0,1:T(8,128)S(1)} %select_bitcast_fusion.1), channel_id=1, replica_groups=mesh['row'=4,'col'=8] {'col'}, dimensions={1}, use_global_device_ids=true | all-gather | bytes 221184 | tf_op jit(solution)/shard_map/all_gather | solution.py:58
  136.6 11.7 %cholesky.16 = f32[128,128]{1,0:T(8,128)S(1)} custom-call(f32[128,128]{1,0:T(8,128)S(1)} %fusion.9), custom_call_target="Cholesky" | custom-call | tf_op jit(solution)/shard_map/jit(cholesky)/cholesky | solution.py:60
  149.0 0.7 fusion.6
  149.6 9.8 %custom-call.7 = f32[1,128,128]{1,2,0:T(8,128)S(1)} custom-call(f32[1,128,128]{2,1,0:T(8,128)S(1)} %fusion.6), custom_call_target="InvertDiagBlocksLowerTriangular" | custom-call | tf_op jit(solution)/shard_map/jit(_solve_triangular)/triangular_solve | solution.py:62
  160.0 1.0 fusion.21
  161.0 9.6 %subtract_convert_fusion = bf16[1536,2048]{1,0:T(8,128)(2,1)} fusion(bf16[1536,2048]{1,0:T(8,128)(2,1)} %param.4, f32[128,2048]{1,0:T(8,128)S(1)} %fusion.21, bf16[128,1536]{1,0:T(8,128)(2,1)S(1)} %gather_fusion.7, pred[128]{0:T(512)(128)(4,1)S(1)} %get-tuple-element.10), kind=kOutput, calls=%fused_computation.9 | convolution fusion | flops 4841472000 | bytes 14024832 | tf_op jit(solution)/shard_map/dot_general | solution.py:69
  170.6 67.6 %all-reduce.3.cloned.1.call-done = (bf16[128,2048]{1,0:T(8,128)(2,1)}, bf16[128,2048]{1,0:T(8,128)(2,1)}) async-done(((bf16[128,2048]{1,0:T(8,128)(2,1)}, bf16[128,2048]{1,0:T(8,128)(2,1)}), (bf16[128,2048]{1,0:T(8,128)(2,1)}, bf16[128,2048]{1,0:T(8,128)(2,1)})) %all-reduce.3.cloned.1.call-update) | async-done | bytes 1048592 | tf_op jit(solution)/shard_map/psum | solution.py:11
  238.2 26.9 %convolution_subtract_fusion = f32[4096,2048]{1,0:T(8,128)} fusion(f32[4096,2048]{1,0:T(8,128)} %param.3, f32[128,2048]{1,0:T(8,128)S(1)} %fusion.21, bf16[128,2048]{1,0:T(8,128)(2,1)} %get-tuple-element.6, bf16[128,2048]{1,0:T(8,128)(2,1)} %get-tuple-element.7), kind=kOutput, calls=%fused_computation.8 | convolution fusion | flops 12895387648 | bytes 69206016 | tf_op jit(solution)/shard_map/dot_general | solution.py:65
  (35 shorter events, 5.5 us)
Async XLA Ops:
  7.2 62.1 %all-gather.5.cloned.1.call-start = ((), (), s32[]{:S(2)}) async-start(), calls=%async_computation.1 | async-start | bytes 1327104 | tf_op jit(solution)/shard_map/all_gather | solution.py:55
  11.4 14.6 %copy-start = (s32[128]{0:T(128)S(1)}, s32[128]{0:T(128)}, u32[]{:S(2)}) copy-start(s32[128]{0:T(128)} %param.5) | copy-start | bytes 1540
  25.2 73.4 %all-gather.3.cloned.1.call-start = ((), (), s32[]{:S(2)}) async-start(), calls=%async_computation | async-start | bytes 3932160 | tf_op jit(solution)/shard_map/all_gather | solution.py:46
  41.6 196.6 %all-reduce.3.cloned.1.call-start = ((), (), s32[]{:S(2)}) async-start(), calls=%async_computation.2 | async-start | bytes 2097152 | tf_op jit(solution)/shard_map/psum | solution.py:11
Sparse Core Ops, SparseCore 0:
  25.3 43.8 all-gather.4
  71.4 27.1 all-gather.2
  159.9 78.2 all-reduce.2
where the time goes:
time: 272 us
  waiting for transfers between devices  122 us (45%)
  matrix products  38 us (14%)
  local copies, waits for them, and re-layouts  35.3 us (13%)
  other arithmetic  31.7 us (12%)
  blocking collectives  30.9 us (11%)
  between operations  14 us (5%)
    psum x1, waiting for transfers between devices, spread(): return lax.psum(block, axis)  67.6 us
    all_gather x1, blocking collectives, on_device(): block_wide = lax.all_gather(own_cols, 'col', axis=1, tiled=True)  30.9 us
    all_gather x1, waiting for transfers between devices, on_device(): weight_wide = lax.all_gather(packed_weight, 'col', axis=1, tiled=True)  27.4 us
    dot_general x1, matrix products, on_device(): lax.dot_general(left_rows, coupling, (((0,), (0,)), ((), ())), precision=...  26.9 us
    all_gather x1, waiting for transfers between devices, on_device(): gathered = lax.all_gather(packed_rows, 'row', axis=0, tiled=True)  26.7 us
    gather x3, local copies, waits for them, and re-layouts, pick_owned(): taken_part = jnp.take(source, local_col, axis=which_axis)  16.9 us
    another operation x3, other arithmetic, on_device(): factor = jnp.linalg.cholesky(removed_block)  12.4 us
    another operation x2, other arithmetic, on_device(): factor_inv = jax.scipy.linalg.solve_triangular(factor, identity, lower=True)  10.5 us
  transfers between devices with their start and end apart: 3, of which 3 were waited for; matrix products, arithmetic and copies ran while one was open for 11% of the time, Pallas kernels for 0%

commit v1 on v0

--- a/solution.py
+++ b/solution.py
@@ -8,7 +8,7 @@
 
 def spread(block, axis, owner):
     block = jnp.where(lax.axis_index(axis) == owner, block, jnp.zeros_like(block))
-    return lax.psum(block, axis)
+    return jax.lax.all_gather(block, axis_name=axis).sum(axis=0)
 
 
 def pick_owned(source, removed, tile_index, tile_size, slot_count, which_axis):

time: 272 us -> 286 us (1.051)
  waiting for transfers between devices: 122 us -> 129 us
  other arithmetic: 31.7 us -> 36.9 us
    all_gather x0 -> x2, waiting for transfers between devices: none -> 75.2 us  [spread(): return jax.lax.all_gather(block, axis_name=axis).sum(axis=0)]
    psum x1 -> x0, waiting for transfers between devices: 67.6 us -> none  [spread(): return lax.psum(block, axis)]
    all_gather x1, waiting for transfers between devices: 26.7 us -> 14.7 us  [on_device(): gathered = lax.all_gather(packed_rows, 'row', axis=0, tiled=True)]
    all_gather x1, waiting for transfers between devices: 27.4 us -> 38.7 us  [on_device(): weight_wide = lax.all_gather(packed_weight, 'col', axis=1, tiled=True)]
    reduce_sum x0 -> x2, other arithmetic: none -> 5.91 us  [spread(): return jax.lax.all_gather(block, axis_name=axis).sum(axis=0)]
  transfers between devices with their start and end apart: 3 -> 4, of which waited for: 3 -> 4; matrix products, arithmetic and copies ran while one was open for 11% -> 22% of each run, Pallas kernels for 0% -> 0%
where the time goes in v1:
time: 286 us; the launch traced here: 285 us
  waiting for transfers between devices  129 us (45%)
  matrix products  37.9 us (13%)
  other arithmetic  36.9 us (13%)
  local copies, waits for them, and re-layouts  35.4 us (12%)
  blocking collectives  31.8 us (11%)
  between operations  14 us (5%)
    all_gather x2, waiting for transfers between devices, spread(): return jax.lax.all_gather(block, axis_name=axis).sum(axis=0)  75.2 us
    all_gather x1, waiting for transfers between devices, on_device(): weight_wide = lax.all_gather(packed_weight, 'col', axis=1, tiled=True)  38.7 us
    all_gather x1, blocking collectives, on_device(): block_wide = lax.all_gather(own_cols, 'col', axis=1, tiled=True)  31.8 us
    dot_general x1, matrix products, on_device(): lax.dot_general(left_rows, coupling, (((0,), (0,)), ((), ())), precision=...  26.6 us
    gather x3, local copies, waits for them, and re-layouts, pick_owned(): taken_part = jnp.take(source, local_col, axis=which_axis)  17.3 us
    all_gather x1, waiting for transfers between devices, on_device(): gathered = lax.all_gather(packed_rows, 'row', axis=0, tiled=True)  14.7 us
    another operation x3, other arithmetic, on_device(): factor = jnp.linalg.cholesky(removed_block)  12.4 us
    another operation x2, other arithmetic, on_device(): factor_inv = jax.scipy.linalg.solve_triangular(factor, identity, lower=True)  10.5 us
  transfers between devices with their start and end apart: 4, of which 4 were waited for; matrix products, arithmetic and copies ran while one was open for 22% of the time, Pallas kernels for 0%

profile of v1, /device:TPU:0, one launch (start us, length us, event | category | flops | bytes accessed | tf_op | source)
XLA Modules:
  0.0 285.3 jit_solution(7393494177504503181)
XLA Ops:
  7.2 1.4 fusion.13
  9.3 1.6 gather_fusion
  12.2 11.8 %gather_fusion.1 = f32[96,2048]{1,0:T(8,128)S(1)} fusion(f32[4096,2048]{1,0:T(8,128)} %param.3, s32[1024]{0:T(1024)S(1)} %pad_clamp_fusion.4), kind=kCustom, calls=%fused_computation.1 | custom fusion | bytes 1573248 | tf_op jit(solution)/shard_map/jit(_take)/gather | solution.py:20
  23.9 1.0 select_select_fusion
  25.7 0.8 gather_fusion.3
  26.5 8.7 %copy.16 = bf16[1536,2048]{0,1:T(8,128)(2,1)} copy(bf16[1536,2048]{1,0:T(8,128)(2,1)} %param.4) | data formatting | bytes 12582912 | tf_op args[1]
  35.2 4.9 %gather_fusion.6 = bf16[48,1536]{1,0:T(8,128)(2,1)S(1)} fusion(bf16[1536,2048]{0,1:T(8,128)(2,1)} %copy.16, s32[1024]{0:T(1024)S(1)} %pad_clamp_fusion.1), kind=kCustom, calls=%fused_computation.6 | custom fusion | bytes 295104 | tf_op jit(solution)/shard_map/jit(_take)/gather | solution.py:20
  40.7 0.8 select_bitcast_fusion
  41.7 14.7 %all-gather.5.cloned.1.call-done = f32[384,2048]{1,0:T(8,128)} async-done(((f32[96,2048]{1,0:T(8,128)}), f32[384,2048]{1,0:T(8,128)}) %all-gather.5.cloned.1.call-update) | async-done | bytes 3145744 | tf_op jit(solution)/shard_map/all_gather | solution.py:46
  56.4 3.3 %gather_fusion.2 = f32[128,2048]{1,0:T(8,128)S(1)} fusion(f32[384,2048]{1,0:T(8,128)} %all-gather.5.cloned.1.call-done, s32[1024]{0:T(1024)S(1)} %pad_clamp_fusion.3), kind=kCustom, calls=%fused_computation.2 | custom fusion | bytes 2097664 | tf_op jit(solution)/shard_map/jit(_take)/gather | solution.py:47
  59.8 1.2 broadcast_select_fusion.2
  61.6 38.7 %all-gather.11.cloned.1.call-done = bf16[1536,384]{0,1:T(8,128)(2,1)} async-done(((bf16[1536,48]{0,1:T(8,128)(2,1)}), bf16[1536,384]{0,1:T(8,128)(2,1)}) %all-gather.11.cloned.1.call-update) | async-done | bytes 1179664 | tf_op jit(solution)/shard_map/all_gather | solution.py:55
  100.3 2.7 gather_fusion.7
  104.1 31.8 %all_gather.20 = f32[128,384]{0,1:T(8,128)S(1)} all-gather(f32[128,48]{0,1:T(8,128)S(1)} %select_bitcast_fusion.1), channel_id=1, replica_groups=mesh['row'=4,'col'=8] {'col'}, dimensions={1}, use_global_device_ids=true | all-gather | bytes 221184 | tf_op jit(solution)/shard_map/all_gather | solution.py:58
  136.9 11.7 %cholesky.16 = f32[128,128]{1,0:T(8,128)S(1)} custom-call(f32[128,128]{1,0:T(8,128)S(1)} %fusion.10), custom_call_target="Cholesky" | custom-call | tf_op jit(solution)/shard_map/jit(cholesky)/cholesky | solution.py:60
  149.3 0.7 fusion.7
  149.9 9.8 %custom-call.7 = f32[1,128,128]{1,2,0:T(8,128)S(1)} custom-call(f32[1,128,128]{2,1,0:T(8,128)S(1)} %fusion.7), custom_call_target="InvertDiagBlocksLowerTriangular" | custom-call | tf_op jit(solution)/shard_map/jit(_solve_triangular)/triangular_solve | solution.py:62
  160.3 1.0 fusion.22
  161.3 9.7 %subtract_convert_fusion = bf16[1536,2048]{1,0:T(8,128)(2,1)} fusion(bf16[1536,2048]{1,0:T(8,128)(2,1)} %param.4, f32[128,2048]{1,0:T(8,128)S(1)} %fusion.22, bf16[128,1536]{1,0:T(8,128)(2,1)S(1)} %gather_fusion.7, pred[128]{0:T(512)(128)(4,1)S(1)} %get-tuple-element.6), kind=kOutput, calls=%fused_computation.9 | convolution fusion | flops 4841472000 | bytes 14024832 | tf_op jit(solution)/shard_map/dot_general | solution.py:69
  171.0 5.0 %all-gather.7.cloned.1.call-done = bf16[8,128,2048]{2,1,0:T(8,128)(2,1)} async-done(((bf16[1,128,2048]{2,1,0:T(8,128)(2,1)}), bf16[8,128,2048]{2,1,0:T(8,128)(2,1)}) %all-gather.7.cloned.1.call-update) | async-done | bytes 4194320 | tf_op jit(solution)/shard_map/all_gather | solution.py:11
  176.0 3.0 %reduce_sum.89 = bf16[128,2048]{1,0:T(8,128)(2,1)S(1)} reduce(bf16[8,128,2048]{2,1,0:T(8,128)(2,1)} %all-gather.7.cloned.1.call-done, bf16[]{:T(256)} %constant.178.clone.1), dimensions={0}, to_apply=%region_3.4 | reduce | flops 1835008 | bytes 4718594 | tf_op jit(solution)/shard_map/reduce_sum | solution.py:11
  179.0 70.2 %all-gather.9.cloned.1.call-done = bf16[8,128,2048]{2,1,0:T(8,128)(2,1)} async-done(((bf16[1,128,2048]{2,1,0:T(8,128)(2,1)}), bf16[8,128,2048]{2,1,0:T(8,128)(2,1)}) %all-gather.9.cloned.1.call-update) | async-done | bytes 4194320 | tf_op jit(solution)/shard_map/all_gather | solution.py:11
  249.2 3.0 %reduce_sum.90 = bf16[128,2048]{1,0:T(8,128)(2,1)S(1)} reduce(bf16[8,128,2048]{2,1,0:T(8,128)(2,1)} %all-gather.9.cloned.1.call-done, bf16[]{:T(256)} %constant.178.clone.1), dimensions={0}, to_apply=%region_4.5 | reduce | flops 1835008 | bytes 4718594 | tf_op jit(solution)/shard_map/reduce_sum | solution.py:11
  252.1 26.6 %convolution_subtract_fusion = f32[4096,2048]{1,0:T(8,128)} fusion(f32[4096,2048]{1,0:T(8,128)} %param.3, f32[128,2048]{1,0:T(8,128)S(1)} %fusion.22, bf16[128,2048]{1,0:T(8,128)(2,1)S(1)} %reduce_sum.90, bf16[128,2048]{1,0:T(8,128)(2,1)S(1)} %reduce_sum.89), kind=kOutput, calls=%fused_computation.8 | convolution fusion | flops 12895387648 | bytes 69206016 | tf_op jit(solution)/shard_map/dot_general | solution.py:65
  (40 shorter events, 7.4 us)
Async XLA Ops:
  7.2 18.6 %copy-start = (s32[128]{0:T(128)S(1)}, s32[128]{0:T(128)}, u32[]{:S(2)}) copy-start(s32[128]{0:T(128)} %param.5) | copy-start | bytes 1540
  7.2 49.2 %all-gather.5.cloned.1.call-start = ((), (), s32[]{:S(2)}) async-start(), calls=%async_computation | async-start | bytes 3932160 | tf_op jit(solution)/shard_map/all_gather | solution.py:46
  25.0 75.3 %all-gather.11.cloned.1.call-start = ((), (), s32[]{:S(2)}) async-start(), calls=%async_computation.3 | async-start | bytes 1327104 | tf_op jit(solution)/shard_map/all_gather | solution.py:55
  41.5 134.5 %all-gather.7.cloned.1.call-start = ((), (), s32[]{:S(2)}) async-start(), calls=%async_computation.1 | async-start | bytes 4718592 | tf_op jit(solution)/shard_map/all_gather | solution.py:11
  61.0 188.2 %all-gather.9.cloned.1.call-start = ((), (), s32[]{:S(2)}) async-start(), calls=%async_computation.2 | async-start | bytes 4718592 | tf_op jit(solution)/shard_map/all_gather | solution.py:11
Sparse Core Ops, SparseCore 0:
  25.1 31.2 all-gather.4
  59.2 41.1 all-gather.10
  103.0 72.9 all-gather.6
  178.0 71.1 all-gather.8
